TPU v7x, 256 devices: a whole 4x4x8 slice. The times are simulated.
256 devices in a mesh: dp: 16 (over x_lo, y, core), mp: 8 (over z), side: 2 (over x_hi).
Axes of the slice: x: 4 (x_hi: 2, x_lo: 2; x = x_hi * 2 + x_lo), y: 4, z: 8, core: 2. Of those that a mesh axis runs over, the one named last changes fastest.
Arguments:
- tokens: bfloat16 [4096, 3072], P('dp', 'mp'), may hold values from -6 to 6
- up_weight: bfloat16 [2, 3072, 6144], P('side', 'dp', 'mp'), may hold values from -0.109375 to 0.109375
- down_weight: bfloat16 [2, 6144, 3072], P('side', 'mp', 'dp'), may hold values from -0.078125 to 0.078125
- mod_table: float32 [2, 50, 3, 3072], P('side'), may hold values from -3 to 3
- timesteps: int32 [16], P('dp'), may hold values from 0 to 49
- valid_counts: int32 [16], replicated, may hold values from 64 to 256, as said below
Outputs:
- block_out: bfloat16 [2, 4096, 3072], P('side', 'dp', 'mp')
- up_grads: float32 [3072, 6144], P(('dp', 'side'), 'mp')
- down_grads: float32 [6144, 3072], P('mp', ('dp', 'side'))
Inputs may be any that keep to these rules, and one draw needn't show every extreme that they name: `valid_counts`: every image has at least 64 valid tokens, and in every draw some image has all 256 valid.
All inputs are finite; a program needn't handle non-finite values.
Results may differ from a plain program's by a relative error of at most 0.018.
Values may be sent and summed in bfloat16 or wider, within the bound.
A program may use at most 64 MiB of HBM per device.

v0:
```python
import jax
import jax.numpy as jnp
from jax import lax
from jax.sharding import PartitionSpec as P


def passed_along(x, axis, by):
    peers = lax.axis_size(axis)
    pairs = [(i, i + by) for i in range(peers) if 0 <= i + by < peers]
    return lax.ppermute(x, axis, pairs)


def gelu_tanh(values):
    return jax.nn.gelu(values, approximate=True)


def shards(tokens, up_weight, down_weight, mod_table, timesteps, valid_counts):
    gathered = lax.all_gather(tokens, "mp", axis=1, tiled=True)
    width = gathered.shape[1]
    shard_width = tokens.shape[1]
    mp_offset = lax.axis_index("mp") * shard_width
    is_student = lax.axis_index("side") == 1
    wide = gathered.astype(jnp.float32)
    average = jnp.mean(wide, axis=-1, keepdims=True)
    centred = wide - average
    variance = jnp.mean(centred * centred, axis=-1, keepdims=True)
    scaled = centred * lax.rsqrt(variance + 1e-06)
    plan = mod_table.shape[1]
    one_hot = (jnp.arange(plan, dtype=jnp.int32)[None, :] == timesteps[0]).astype(jnp.float32)
    modulation = jnp.dot(
        one_hot,
        mod_table[0].reshape(plan, 3 * width),
        precision=lax.Precision.HIGHEST,
        preferred_element_type=jnp.float32,
    ).reshape(3, width)
    normed = (scaled * (1.0 + modulation[1]) + modulation[0]).astype(jnp.bfloat16)
    gate_row = modulation[2]
    hidden_pre = jnp.dot(
        normed,
        lax.all_gather(up_weight[0], "dp", axis=0, tiled=True),
        preferred_element_type=jnp.float32,
    )
    hidden_act = gelu_tanh(hidden_pre).astype(jnp.bfloat16)
    down_full = lax.all_gather(down_weight[0], "dp", axis=1, tiled=True)
    partial_value = jnp.dot(hidden_act, down_full, preferred_element_type=jnp.float32)
    positions = jnp.arange(normed.shape[0], dtype=jnp.int32)
    own_count = lax.dynamic_index_in_dim(valid_counts, lax.axis_index("dp"), 0, keepdims=False)
    valid_col = (positions < own_count).astype(jnp.float32)[:, None]
    valid_total = jnp.sum(valid_counts).astype(jnp.float32)
    mixed = lax.psum(partial_value.astype(jnp.bfloat16), "mp").astype(jnp.float32)
    out_full = (wide + gate_row * mixed).astype(jnp.bfloat16)
    out_local = lax.dynamic_slice_in_dim(out_full, mp_offset, shard_width, 1)
    other_full = passed_along(out_full, "side", 1)
    differ = out_full.astype(jnp.float32) - other_full.astype(jnp.float32)
    grad_out = (gate_row * differ * valid_col / jnp.sqrt(valid_total)).astype(jnp.bfloat16)

    def backprop():
        grad_act = lax.dot_general(
            grad_out, down_full, (((1,), (1,)), ((), ())), preferred_element_type=jnp.float32
        )
        unused, pullback = jax.vjp(gelu_tanh, hidden_pre)
        return pullback(grad_act)[0].astype(jnp.bfloat16)

    def no_backprop():
        return jnp.zeros(hidden_pre.shape, jnp.bfloat16)

    grad_pre = lax.cond(is_student, backprop, no_backprop)
    ff_width = hidden_act.shape[1]

    def product():
        return lax.dot_general(
            normed, grad_pre, (((0,), (0,)), ((), ())), preferred_element_type=jnp.float32
        )

    def nothing():
        return jnp.zeros(
            (width // lax.axis_size(("dp", "side")) * lax.axis_size(("dp", "side")), ff_width),
            jnp.float32,
        )

    up_share = lax.psum_scatter(
        lax.cond(is_student, product, nothing).astype(jnp.bfloat16),
        ("dp", "side"),
        scatter_dimension=0,
        tiled=True,
    ).astype(jnp.float32)

    def down_product():
        return lax.dot_general(
            hidden_act, grad_out, (((0,), (0,)), ((), ())), preferred_element_type=jnp.float32
        )

    def down_nothing():
        return jnp.zeros((ff_width, width), jnp.float32)

    down_term = lax.cond(is_student, down_product, down_nothing)
    down_share = lax.psum_scatter(
        down_term.astype(jnp.bfloat16), ("dp", "side"), scatter_dimension=1, tiled=True
    ).astype(jnp.float32)
    return (out_local[None], up_share, down_share)


def solution(mesh):
    placed = (
        P("dp", "mp"),
        P("side", "dp", "mp"),
        P("side", "mp", "dp"),
        P("side", None, None, None),
        P("dp"),
        P(),
    )
    return jax.shard_map(
        shards,
        mesh=mesh,
        in_specs=placed,
        out_specs=(P("side", "dp", "mp"), P(("dp", "side"), "mp"), P("mp", ("dp", "side"))),
        check_vma=False,
    )
```

profile of v0, /device:TPU:1, one launch (start us, length us, event | category | flops | bytes accessed | tf_op | source)
XLA Modules:
  0.0 593.4 jit_solution(2284106600337096998)
XLA Ops:
  7.2 0.0 all-gather.6.cloned.1.call-start
  7.2 0.7 all-gather.6.cloned.1.call-update
  7.9 0.0 all-gather.8.cloned.1.call-start
  7.9 0.7 all-gather.8.cloned.1.call-update
  8.6 0.0 all-gather.10.cloned.1.call-start
  8.7 0.7 all-gather.10.cloned.1.call-update
  9.4 0.0 all-reduce.2.cloned.1.call-start
  9.4 6.5 %reduce = f32[50,3,3072]{2,1,0:T(4,128)S(1)} reduce(f32[1,50,3,3072]{3,0,2,1:T(1,128)} %param.15, f32[]{:T(128)} %constant.65), dimensions={0}, to_apply=%param.15.reduce_sub_computation | reduce | bytes 3686404 | tf_op args[3]
  15.9 0.5 pad
  16.5 1.2 copy.14
  18.3 0.8 fusion.24
  19.1 29.2 %all-gather.6.cloned.1.call-done = bf16[256,3072]{1,0:T(8,128)(2,1)} async-done(((bf16[256,384]{1,0:T(8,128)(2,1)}), bf16[256,3072]{1,0:T(8,128)(2,1)}) %all-gather.6.cloned.1.call-update) | async-done | bytes 1572880 | tf_op jit(solution)/shard_map/all_gather | solution.py:18
  48.2 0.0 copy-start
  48.2 1.8 convert_reduce_fusion
  50.1 2.0 fusion.11
  52.0 0.0 copy-done
  52.0 0.8 fusion.14
  52.8 41.7 %all-gather.8.cloned.1.call-done = bf16[1,3072,768]{2,1,0:T(8,128)(2,1)} async-done(((bf16[1,192,768]{2,1,0:T(8,128)(2,1)}), bf16[1,3072,768]{2,1,0:T(8,128)(2,1)}) %all-gather.8.cloned.1.call-update) | async-done | bytes 4718608 | tf_op jit(solution)/shard_map/all_gather | solution.py:40
  94.5 4.6 fusion.23
  99.2 0.0 copy-start.1
  99.2 37.7 %all-gather.10.cloned.1.call-done = bf16[1,768,3072]{1,2,0:T(8,128)(2,1)} async-done(((bf16[1,768,192]{1,2,0:T(8,128)(2,1)}), bf16[1,768,3072]{1,2,0:T(8,128)(2,1)}) %all-gather.10.cloned.1.call-update) | async-done | bytes 4718608 | tf_op jit(solution)/shard_map/all_gather | solution.py:44
  136.9 4.9 convolution_convert_fusion
  141.8 0.0 copy-done.1
  141.8 0.0 copy-start.3
  141.8 0.0 all-reduce.2.cloned.1.call-update
  141.8 0.2 reduce-scatter.3.cloned.1.call-start
  142.1 74.3 %all-reduce.2.cloned.1.call-done = bf16[256,3072]{1,0:T(8,128)(2,1)} async-done(((bf16[256,3072]{1,0:T(8,128)(2,1)}), bf16[256,3072]{1,0:T(8,128)(2,1)}) %all-reduce.2.cloned.1.call-update) | async-done | bytes 1572880 | tf_op jit(solution)/shard_map/psum | solution.py:50
  216.3 3.1 fusion.15
  219.5 5.8 collective-permute-start
  225.2 0.0 copy-done.3
  225.2 0.6 reduce_sum.29
  226.6 0.6 dynamic_slice.8
  227.2 0.6 compare_convert_fusion
  227.8 25.6 %collective-permute-done = bf16[256,3072]{1,0:T(8,128)(2,1)} collective-permute-done((bf16[256,3072]{1,0:T(8,128)(2,1)}, bf16[256,3072]{1,0:T(8,128)(2,1)}, u32[]{:S(2)}, u32[]{:S(2)}) %collective-permute-start) | collective-permute-done | bytes 1572896 | tf_op jit(solution)/shard_map/ppermute | solution.py:10
  253.4 2.6 divide_convert_fusion
  256.0 0.1 conditional.3
  256.1 2.5 conditional.4
  256.1 2.5 broadcast.75
  258.6 0.0 copy-start.2
  258.6 0.0 reduce-scatter.3.cloned.1.call-update
  258.6 0.0 reduce-scatter.5.cloned.1.call-start
  258.6 0.9 copy-done.2
  259.6 2.8 conditional.5
  259.6 2.8 broadcast.76
  262.4 6.6 %copy.12 = bf16[768,3072]{0,1:T(8,128)(2,1)} copy(bf16[768,3072]{1,0:T(8,128)(2,1)} %get-tuple-element.43) | data formatting | bytes 9437184 | tf_op jit(solution)/shard_map/cond | solution.py:96
  269.0 0.0 reduce-scatter.5.cloned.1.call-update
  269.0 1.6 dynamic-slice_bitcast_fusion
  270.6 155.2 %reduce-scatter.3.cloned.1.call-done = bf16[96,768]{1,0:T(8,128)(2,1)} async-done(((bf16[3072,768]{1,0:T(8,128)(2,1)}), bf16[96,768]{1,0:T(8,128)(2,1)}) %reduce-scatter.3.cloned.1.call-update) | async-done | bytes 147472 | tf_op jit(solution)/shard_map/reduce_scatter | solution.py:81
  425.9 1.6 convert_element_type.71
  427.5 157.4 %reduce-scatter.5.cloned.1.call-done = bf16[768,96]{0,1:T(8,128)(2,1)} async-done(((bf16[768,3072]{0,1:T(8,128)(2,1)}), bf16[768,96]{0,1:T(8,128)(2,1)}) %reduce-scatter.5.cloned.1.call-update) | async-done | bytes 147472 | tf_op jit(solution)/shard_map/reduce_scatter | solution.py:97
  584.9 1.6 convert_element_type.73
  (4 shorter events, 0.1 us)
Async XLA Ops:
  7.2 41.1 %all-gather.6.cloned.1.call-start = ((), (), s32[]{:S(2)}) async-start(), calls=%async_computation.2 | async-start | bytes 1769472 | tf_op jit(solution)/shard_map/all_gather | solution.py:18
  7.9 86.6 %all-gather.8.cloned.1.call-start = ((), (), s32[]{:S(2)}) async-start(), calls=%async_computation.6 | async-start | bytes 5013504 | tf_op jit(solution)/shard_map/all_gather | solution.py:40
  8.6 128.2 %all-gather.10.cloned.1.call-start = ((), (), s32[]{:S(2)}) async-start(), calls=%async_computation.7 | async-start | bytes 5013504 | tf_op jit(solution)/shard_map/all_gather | solution.py:44
  9.4 207.0 %all-reduce.2.cloned.1.call-start = ((), (), s32[]{:S(2)}) async-start(), calls=%async_computation.3 | async-start | bytes 3145728 | tf_op jit(solution)/shard_map/psum | solution.py:50
  48.2 3.8 copy-start
  99.2 42.7 %copy-start.1 = (bf16[256,768]{1,0:T(8,128)(2,1)}, bf16[256,768]{1,0:T(8,128)(2,1)S(1)}, u32[]{:S(2)}) copy-start(bf16[256,768]{1,0:T(8,128)(2,1)S(1)} %get-tuple-element.39) | copy-start | bytes 1179652
  141.8 83.4 %copy-start.3 = (s32[16]{0:T(128)S(1)}, s32[16]{0:T(128)}, u32[]{:S(2)}) copy-start(s32[16]{0:T(128)} %param.17) | copy-start | bytes 196
  141.8 284.0 %reduce-scatter.3.cloned.1.call-start = ((), (), s32[]{:S(2)}) async-start(), calls=%async_computation.4 | async-start | bytes 4866048 | tf_op jit(solution)/shard_map/reduce_scatter | solution.py:81
  219.5 34.0 %collective-permute-start = (bf16[256,3072]{1,0:T(8,128)(2,1)}, bf16[256,3072]{1,0:T(8,128)(2,1)}, u32[]{:S(2)}, u32[]{:S(2)}) collective-permute-start(bf16[256,3072]{1,0:T(8,128)(2,1)} %fusion.15), channel_id=1, source_target_pairs={{0,1},{2,3},{4,5},{6,7},{8,9},{10,11},{12,13},{14,15},{16,17},{18,... | collective-permute-start | bytes 4718600 | tf_op jit(solution)/shard_map/ppermute | solution.py:10
  258.6 1.0 copy-start.2
  258.6 326.3 %reduce-scatter.5.cloned.1.call-start = ((), (), s32[]{:S(2)}) async-start(), calls=%async_computation.5 | async-start | bytes 4866048 | tf_op jit(solution)/shard_map/reduce_scatter | solution.py:97
Sparse Core Ops, SparseCore 0:
  9.8 38.4 all-gather.5
  50.1 44.3 all-gather.7
  96.4 40.4 all-gather.9
  142.0 74.3 all-reduce.1
  258.7 167.0 reduce-scatter.2
  428.2 156.6 reduce-scatter.4
where the time goes:
time: 594 us; the launch traced here: 593 us
  waiting for transfers between devices  523 us (88%)
  other arithmetic  21.3 us (4%)
  local copies, waits for them, and re-layouts  16.8 us (3%)
  between operations  15.5 us (3%)
  matrix products  10.3 us (2%)
  starting transfers between devices  6.19 us (1%)
    reduce_scatter x1, waiting for transfers between devices, shards(): lax.psum_scatter(down_term.astype(jnp.bfloat16), ('dp', 'side'), scatter_...  157 us
    reduce_scatter x1, waiting for transfers between devices, shards(): lax.psum_scatter(lax.cond(is_student, product, nothing).astype(jnp.bfloat...  155 us
    psum x1, waiting for transfers between devices, shards(): lax.psum(partial_value.astype(jnp.bfloat16), 'mp').astype(jnp.float32)  74.3 us
    all_gather x1, waiting for transfers between devices, shards(): lax.all_gather(up_weight[0], 'dp', axis=0, tiled=True)  41.7 us
    all_gather x1, waiting for transfers between devices, shards(): down_full = lax.all_gather(down_weight[0], 'dp', axis=1, tiled=True)  37.7 us
    all_gather x1, waiting for transfers between devices, shards(): gathered = lax.all_gather(tokens, 'mp', axis=1, tiled=True)  29.2 us
    ppermute x1, waiting for transfers between devices, passed_along(): return lax.ppermute(x, axis, pairs)  25.6 us
  transfers between devices with their start and end apart: 7, of which 7 were waited for; matrix products, arithmetic and copies ran while one was open for 6% of the time, Pallas kernels for 0%

commit v1 on v0

--- a/solution.py
+++ b/solution.py
@@ -37,7 +37,9 @@
     gate_row = modulation[2]
     hidden_pre = jnp.dot(
         normed,
-        lax.all_gather(up_weight[0], "dp", axis=0, tiled=True),
+        jnp.concatenate(
+            lax.all_to_all(jnp.stack([up_weight[0]] * lax.axis_size("dp")), "dp", 0, 0), axis=0
+        ),
         preferred_element_type=jnp.float32,
     )
     hidden_act = gelu_tanh(hidden_pre).astype(jnp.bfloat16)

time: 594 us -> 566 us (0.953)
  waiting for transfers between devices: 523 us -> 484 us
  starting transfers between devices: 6.19 us -> 13.6 us
    all_gather x1 -> x0, waiting for transfers between devices: 41.7 us -> none  [shards(): lax.all_gather(up_weight[0], 'dp', axis=0, tiled=True)]
    all_to_all x0 -> x1, waiting for transfers between devices: none -> 40 us  [shards(): lax.all_to_all(jnp.stack([up_weight[0]] * lax.axis_size('dp')), 'dp', 0, 0)]
    all_gather x1, waiting for transfers between devices: 37.7 us -> 8.62 us  [shards(): down_full = lax.all_gather(down_weight[0], 'dp', axis=1, tiled=True)]
    all_gather x1, waiting for transfers between devices: 29.2 us -> 19.7 us  [shards(): gathered = lax.all_gather(tokens, 'mp', axis=1, tiled=True)]
    all_to_all x0 -> x1, starting transfers between devices: none -> 7.51 us  [shards(): lax.all_to_all(jnp.stack([up_weight[0]] * lax.axis_size('dp')), 'dp', 0, 0)]
where the time goes in v1:
time: 566 us; the launch traced here: 565 us
  waiting for transfers between devices  484 us (86%)
  other arithmetic  21.4 us (4%)
  local copies, waits for them, and re-layouts  20.4 us (4%)
  between operations  15.2 us (3%)
  starting transfers between devices  13.6 us (2%)
  matrix products  10.4 us (2%)
    reduce_scatter x1, waiting for transfers between devices, shards(): lax.psum_scatter(down_term.astype(jnp.bfloat16), ('dp', 'side'), scatter_...  158 us
    reduce_scatter x1, waiting for transfers between devices, shards(): lax.psum_scatter(lax.cond(is_student, product, nothing).astype(jnp.bfloat...  156 us
    psum x1, waiting for transfers between devices, shards(): lax.psum(partial_value.astype(jnp.bfloat16), 'mp').astype(jnp.float32)  75.6 us
    all_to_all x1, waiting for transfers between devices, shards(): lax.all_to_all(jnp.stack([up_weight[0]] * lax.axis_size('dp')), 'dp', 0, 0)  40 us
    ppermute x1, waiting for transfers between devices, passed_along(): return lax.ppermute(x, axis, pairs)  25.6 us
    all_gather x1, waiting for transfers between devices, shards(): gathered = lax.all_gather(tokens, 'mp', axis=1, tiled=True)  19.7 us
  transfers between devices with their start and end apart: 7, of which 7 were waited for; matrix products, arithmetic and copies ran while one was open for 6% of the time, Pallas kernels for 0%

profile of v1, /device:TPU:1, one launch (start us, length us, event | category | flops | bytes accessed | tf_op | source)
XLA Modules:
  0.0 565.5 jit_solution(12662003448927047458)
XLA Ops:
  7.2 0.0 all-gather.4.cloned.1.call-start
  7.2 0.7 all-gather.4.cloned.1.call-update
  7.9 0.0 all-gather.6.cloned.1.call-start
  7.9 0.7 all-gather.6.cloned.1.call-update
  8.6 3.6 stack.3
  12.3 7.5 %all-to-all-start = ((bf16[16,192,768]{2,1,0:T(8,128)(2,1)}), bf16[16,192,768]{2,1,0:T(8,128)(2,1)}, u32[]{:S(2)}, u32[]{:S(2)}) async-start(bf16[16,192,768]{2,1,0:T(8,128)(2,1)} %stack.3), calls=%async_computation | async-start | bytes 9437184 | tf_op jit(solution)/shard_map/all_to_all | solution.py:41
  19.8 0.0 all-reduce.2.cloned.1.call-start
  19.8 6.5 %reduce = f32[50,3,3072]{2,1,0:T(4,128)S(1)} reduce(f32[1,50,3,3072]{3,0,2,1:T(1,128)} %param.15, f32[]{:T(128)} %constant.65), dimensions={0}, to_apply=%param.15.reduce_sub_computation | reduce | bytes 3686404 | tf_op args[3]
  26.4 0.5 pad
  26.9 1.2 copy.14
  28.7 0.8 fusion.22
  29.5 19.7 %all-gather.4.cloned.1.call-done = bf16[256,3072]{1,0:T(8,128)(2,1)} async-done(((bf16[256,384]{1,0:T(8,128)(2,1)}), bf16[256,3072]{1,0:T(8,128)(2,1)}) %all-gather.4.cloned.1.call-update) | async-done | bytes 1572880 | tf_op jit(solution)/shard_map/all_gather | solution.py:18
  49.2 0.0 copy-start
  49.2 1.8 convert_reduce_fusion
  51.0 2.0 fusion.9
  53.0 0.0 copy-done
  53.0 0.8 fusion.12
  53.8 40.0 %all-to-all-done = bf16[16,192,768]{2,1,0:T(8,128)(2,1)} async-done(((bf16[16,192,768]{2,1,0:T(8,128)(2,1)}), bf16[16,192,768]{2,1,0:T(8,128)(2,1)}, u32[]{:S(2)}, u32[]{:S(2)}) %all-to-all-start) | async-done | bytes 4718624 | tf_op jit(solution)/shard_map/all_to_all | solution.py:41
  93.8 4.7 fusion.21
  98.4 0.0 copy-start.1
  98.4 8.6 %all-gather.6.cloned.1.call-done = bf16[1,768,3072]{1,2,0:T(8,128)(2,1)} async-done(((bf16[1,768,192]{1,2,0:T(8,128)(2,1)}), bf16[1,768,3072]{1,2,0:T(8,128)(2,1)}) %all-gather.6.cloned.1.call-update) | async-done | bytes 4718608 | tf_op jit(solution)/shard_map/all_gather | solution.py:46
  107.1 4.9 convolution_convert_fusion
  112.0 0.0 copy-done.1
  112.0 0.0 copy-start.3
  112.0 0.0 all-reduce.2.cloned.1.call-update
  112.0 0.2 reduce-scatter.3.cloned.1.call-start
  112.2 75.6 %all-reduce.2.cloned.1.call-done = bf16[256,3072]{1,0:T(8,128)(2,1)} async-done(((bf16[256,3072]{1,0:T(8,128)(2,1)}), bf16[256,3072]{1,0:T(8,128)(2,1)}) %all-reduce.2.cloned.1.call-update) | async-done | bytes 1572880 | tf_op jit(solution)/shard_map/psum | solution.py:52
  187.9 3.1 fusion.13
  191.0 5.8 %collective-permute-start = (bf16[256,3072]{1,0:T(8,128)(2,1)}, bf16[256,3072]{1,0:T(8,128)(2,1)}, u32[]{:S(2)}, u32[]{:S(2)}) collective-permute-start(bf16[256,3072]{1,0:T(8,128)(2,1)} %fusion.13), channel_id=1, source_target_pairs={{0,1},{2,3},{4,5},{6,7},{8,9},{10,11},{12,13},{14,15},{16,17},{18,... | collective-permute-start | bytes 4718600 | tf_op jit(solution)/shard_map/ppermute | solution.py:10
  196.8 0.0 copy-done.3
  196.8 0.6 reduce_sum.29
  198.1 0.6 dynamic_slice.8
  198.7 0.6 compare_convert_fusion
  199.3 25.6 %collective-permute-done = bf16[256,3072]{1,0:T(8,128)(2,1)} collective-permute-done((bf16[256,3072]{1,0:T(8,128)(2,1)}, bf16[256,3072]{1,0:T(8,128)(2,1)}, u32[]{:S(2)}, u32[]{:S(2)}) %collective-permute-start) | collective-permute-done | bytes 1572896 | tf_op jit(solution)/shard_map/ppermute | solution.py:10
  225.0 2.6 divide_convert_fusion
  227.5 0.1 conditional.3
  227.6 2.5 conditional.4
  227.6 2.5 broadcast.76
  230.1 0.0 copy-start.2
  230.1 0.0 reduce-scatter.3.cloned.1.call-update
  230.1 0.0 reduce-scatter.5.cloned.1.call-start
  230.2 0.9 copy-done.2
  231.1 2.8 conditional.5
  231.1 2.8 broadcast.77
  233.9 6.6 %copy.12 = bf16[768,3072]{0,1:T(8,128)(2,1)} copy(bf16[768,3072]{1,0:T(8,128)(2,1)} %get-tuple-element.43) | data formatting | bytes 9437184 | tf_op jit(solution)/shard_map/cond | solution.py:98
  240.5 0.0 reduce-scatter.5.cloned.1.call-update
  240.5 1.6 dynamic-slice_bitcast_fusion
  242.2 155.5 %reduce-scatter.3.cloned.1.call-done = bf16[96,768]{1,0:T(8,128)(2,1)} async-done(((bf16[3072,768]{1,0:T(8,128)(2,1)}), bf16[96,768]{1,0:T(8,128)(2,1)}) %reduce-scatter.3.cloned.1.call-update) | async-done | bytes 147472 | tf_op jit(solution)/shard_map/reduce_scatter | solution.py:83
  397.7 1.6 convert_element_type.71
  399.3 158.0 %reduce-scatter.5.cloned.1.call-done = bf16[768,96]{0,1:T(8,128)(2,1)} async-done(((bf16[768,3072]{0,1:T(8,128)(2,1)}), bf16[768,96]{0,1:T(8,128)(2,1)}) %reduce-scatter.5.cloned.1.call-update) | async-done | bytes 147472 | tf_op jit(solution)/shard_map/reduce_scatter | solution.py:99
  557.3 1.6 convert_element_type.73
  (4 shorter events, 0.1 us)
Async XLA Ops:
  7.2 42.0 %all-gather.4.cloned.1.call-start = ((), (), s32[]{:S(2)}) async-start(), calls=%async_computation.3 | async-start | bytes 1769472 | tf_op jit(solution)/shard_map/all_gather | solution.py:18
  7.9 99.2 %all-gather.6.cloned.1.call-start = ((), (), s32[]{:S(2)}) async-start(), calls=%async_computation.7 | async-start | bytes 5013504 | tf_op jit(solution)/shard_map/all_gather | solution.py:46
  12.3 81.5 %all-to-all-start = ((bf16[16,192,768]{2,1,0:T(8,128)(2,1)}), bf16[16,192,768]{2,1,0:T(8,128)(2,1)}, u32[]{:S(2)}, u32[]{:S(2)}) async-start(bf16[16,192,768]{2,1,0:T(8,128)(2,1)} %stack.3), calls=%async_computation | async-start | bytes 9437184 | tf_op jit(solution)/shard_map/all_to_all | solution.py:41
  19.8 168.1 %all-reduce.2.cloned.1.call-start = ((), (), s32[]{:S(2)}) async-start(), calls=%async_computation.4 | async-start | bytes 3145728 | tf_op jit(solution)/shard_map/psum | solution.py:52
  49.2 3.8 copy-start
  98.4 13.5 %copy-start.1 = (bf16[256,768]{1,0:T(8,128)(2,1)}, bf16[256,768]{1,0:T(8,128)(2,1)S(1)}, u32[]{:S(2)}) copy-start(bf16[256,768]{1,0:T(8,128)(2,1)S(1)} %get-tuple-element.39) | copy-start | bytes 1179652
  112.0 84.8 %copy-start.3 = (s32[16]{0:T(128)S(1)}, s32[16]{0:T(128)}, u32[]{:S(2)}) copy-start(s32[16]{0:T(128)} %param.17) | copy-start | bytes 196
  112.0 285.7 %reduce-scatter.3.cloned.1.call-start = ((), (), s32[]{:S(2)}) async-start(), calls=%async_computation.5 | async-start | bytes 4866048 | tf_op jit(solution)/shard_map/reduce_scatter | solution.py:83
  191.0 34.0 %collective-permute-start = (bf16[256,3072]{1,0:T(8,128)(2,1)}, bf16[256,3072]{1,0:T(8,128)(2,1)}, u32[]{:S(2)}, u32[]{:S(2)}) collective-permute-start(bf16[256,3072]{1,0:T(8,128)(2,1)} %fusion.13), channel_id=1, source_target_pairs={{0,1},{2,3},{4,5},{6,7},{8,9},{10,11},{12,13},{14,15},{16,17},{18,... | collective-permute-start | bytes 4718600 | tf_op jit(solution)/shard_map/ppermute | solution.py:10
  230.1 1.0 copy-start.2
  230.1 327.2 %reduce-scatter.5.cloned.1.call-start = ((), (), s32[]{:S(2)}) async-start(), calls=%async_computation.6 | async-start | bytes 4866048 | tf_op jit(solution)/shard_map/reduce_scatter | solution.py:99
Sparse Core Ops, SparseCore 0:
  9.8 39.3 all-gather.3
  51.0 56.0 all-gather.5
  112.1 75.7 all-reduce.1
  230.2 167.4 reduce-scatter.2
  400.1 157.1 reduce-scatter.4
